TPU v7x, 512 devices: a whole 4x8x8 slice. The times are simulated.
512 devices in a mesh: layer: 8 (over z_hi, core), feat: 64 (over x, y, z_lo).
Axes of the slice: x: 4, y: 8, z: 8 (z_hi: 4, z_lo: 2; z = z_hi * 2 + z_lo), core: 2. Of those that a mesh axis runs over, the one named last changes fastest.
Arguments:
- source: float32 [8, 256, 2048], P('layer', 'feat'), may hold values from -6 to 6
- w_enc: bfloat16 [8, 2048, 24576], P('layer', None, 'feat'), may hold values from -0.125 to 0.125
- b_enc: float32 [8, 24576], P('layer', 'feat'), may hold values from -3 to 3
- threshold: float32 [8, 24576], P('layer', 'feat'), may hold values from 0.2 to 2
- dec_self: bfloat16 [8, 24576, 2048], P('layer', 'feat'), may hold values from -0.0390625 to 0.0390625
- dec_next: bfloat16 [8, 24576, 2048], P('layer', 'feat'), may hold values from -0.0390625 to 0.0390625
- target: float32 [8, 256, 2048], P('layer', 'feat'), may hold values from -3 to 3
Outputs:
- residual: float32 [8, 256, 2048], P('layer', 'feat')
All inputs are finite; a program needn't handle non-finite values.
Results may differ from a plain program's by a relative error of at most 0.0038.
Values may be sent and summed in bfloat16 or wider, within the bound.
A program may use at most 64 MiB of HBM per device.

v0:
```python
import jax
import jax.numpy as jnp
from jax import lax
from jax.sharding import PartitionSpec as P


def passed_along(value, axis, steps):
    count = lax.axis_size(axis)
    first, last = (max(0, -steps), min(count, count - steps))
    return lax.ppermute(value, axis, [(source, source + steps) for source in range(first, last)])


def body(source, w_enc, b_enc, threshold, dec_self, dec_next, target):
    rows = source[0]
    scale = lax.rsqrt(jnp.mean(rows * rows, axis=1, keepdims=True) + 1e-05)
    normed = (rows * scale).astype(jnp.bfloat16)
    encoder = w_enc[0]
    bias = b_enc[0]
    limits = threshold[0]
    own_dec = dec_self[0]
    after_dec = dec_next[0]
    pre = (
        jnp.dot(
            lax.all_gather(normed, "feat", axis=0, tiled=True),
            encoder,
            preferred_element_type=jnp.float32,
        )
        + bias
    )
    codes = (pre * jax.nn.sigmoid((pre - limits) / 0.1)).astype(jnp.bfloat16)
    block = codes
    own = lax.psum_scatter(
        jnp.dot(block, own_dec, preferred_element_type=jnp.float32),
        "feat",
        scatter_dimension=0,
        tiled=True,
    )
    block = codes
    carried = lax.psum_scatter(
        jnp.dot(block, after_dec, preferred_element_type=jnp.float32),
        "feat",
        scatter_dimension=0,
        tiled=True,
    )
    moved = passed_along(carried, "layer", 1)
    recon = own + moved
    return (recon - target[0])[None]


def solution(mesh):
    return jax.shard_map(
        body,
        mesh=mesh,
        in_specs=(
            P("layer", "feat", None),
            P("layer", None, "feat"),
            P("layer", "feat"),
            P("layer", "feat"),
            P("layer", "feat", None),
            P("layer", "feat", None),
            P("layer", "feat", None),
        ),
        out_specs=P("layer", "feat", None),
        check_vma=False,
    )
```

profile of v0, /device:TPU:1, one launch (start us, length us, event | category | flops | bytes accessed | tf_op | source)
XLA Modules:
  0.0 961.9 jit_solution(8847555858661059731)
XLA Ops:
  6.5 0.0 copy-start
  6.5 0.0 all-gather.3.cloned.1.call-start
  6.5 1.0 fusion.13
  7.6 1.4 fusion.15
  9.0 0.0 all-gather.3.cloned.1.call-update
  9.0 0.0 all-reduce.5.cloned.1.call-start
  9.1 0.7 reduce
  9.8 0.7 reduce.1
  10.5 258.5 %all-gather.3.cloned.1.call-done = bf16[64,4,2048]{2,1,0:T(4,128)(2,1)} async-done(((bf16[1,4,2048]{2,1,0:T(4,128)(2,1)}), bf16[64,4,2048]{2,1,0:T(4,128)(2,1)}) %all-gather.3.cloned.1.call-update) | async-done | bytes 1048592 | tf_op jit(solution)/shard_map/all_gather | solution.py:24
  269.0 1.3 reshape.9
  270.3 2.2 multiply_convert_fusion
  272.5 0.0 copy-done
  272.5 0.0 copy-start.1
  272.5 2.0 fusion
  274.6 0.0 copy-done.1
  274.6 2.1 fusion.2
  276.6 0.0 copy-start.2
  276.6 0.0 all-reduce.5.cloned.1.call-update
  276.6 1.3 dynamic-slice
  278.6 621.6 %all-reduce.5.cloned.1.call-done = (f32[256,2048]{1,0:T(8,128)}, f32[256,2048]{1,0:T(8,128)}) async-done(((f32[256,2048]{1,0:T(8,128)}, f32[256,2048]{1,0:T(8,128)}), (f32[256,2048]{1,0:T(8,128)}, f32[256,2048]{1,0:T(8,128)})) %all-reduce.5.cloned.1.call-update) | async-done | bytes 4194320
  900.1 0.8 constant_dynamic-slice_fusion
  901.0 51.6 %collective-permute-start = (f32[4,2048]{1,0:T(4,128)S(1)}, f32[4,2048]{1,0:T(4,128)S(1)}, u32[]{:S(2)}, u32[]{:S(2)}) collective-permute-start(f32[4,2048]{1,0:T(4,128)S(1)} %constant_dynamic-slice_fusion), channel_id=1, source_target_pairs={{0,64},{64,128},{128,192},{192,256},{256,320},{320,384},{384,448},... | collective-permute-start | bytes 98312 | tf_op jit(solution)/shard_map/ppermute | solution.py:10
  952.6 1.0 collective-permute-done
  953.6 0.0 copy-done.2
  953.6 1.5 fusion.12
  (1 shorter events, 0.0 us)
Async XLA Ops:
  6.5 266.0 %copy-start = (bf16[1,384,2048]{2,1,0:T(8,128)(2,1)S(1)}, bf16[1,384,2048]{2,1,0:T(8,128)(2,1)}, u32[]{:S(2)}) copy-start(bf16[1,384,2048]{2,1,0:T(8,128)(2,1)} %param.12) | copy-start | bytes 4718596
  6.5 262.4 %all-gather.3.cloned.1.call-start = ((), (), s32[]{:S(2)}) async-start(), calls=%async_computation | async-start | bytes 1064960 | tf_op jit(solution)/shard_map/all_gather | solution.py:24
  9.0 891.1 %all-reduce.5.cloned.1.call-start = ((), (), s32[]{:S(2)}) async-start(), calls=%async_computation.1 | async-start | bytes 8388608
  272.5 2.1 copy-start.1
  276.6 677.0 %copy-start.2 = (f32[1,4,2048]{2,1,0:T(4,128)S(1)}, f32[1,4,2048]{2,1,0:T(4,128)}, u32[]{:S(2)}) copy-start(f32[1,4,2048]{2,1,0:T(4,128)} %param.13) | copy-start | bytes 98308
  901.0 52.6 %collective-permute-start = (f32[4,2048]{1,0:T(4,128)S(1)}, f32[4,2048]{1,0:T(4,128)S(1)}, u32[]{:S(2)}, u32[]{:S(2)}) collective-permute-start(f32[4,2048]{1,0:T(4,128)S(1)} %constant_dynamic-slice_fusion), channel_id=1, source_target_pairs={{0,64},{64,128},{128,192},{192,256},{256,320},{320,384},{384,448},... | collective-permute-start | bytes 98312 | tf_op jit(solution)/shard_map/ppermute | solution.py:10
Sparse Core Ops, SparseCore 0:
  9.4 259.4 all-gather.2
  276.8 623.3 all-reduce.4
where the time goes:
time: 962 us
  waiting for transfers between devices  881 us (92%)
  starting transfers between devices  51.7 us (5%)
  between operations  14.1 us (1%)
    unnamed x3, waiting for transfers between devices  622 us
    all_gather x1, waiting for transfers between devices, body(): lax.all_gather(normed, 'feat', axis=0, tiled=True)  258 us
    ppermute x1, starting transfers between devices, passed_along(): lax.ppermute(value, axis, [(source, source + steps) for source in range(f...  51.6 us
  transfers between devices with their start and end apart: 3, of which 3 were waited for; matrix products, arithmetic and copies ran while one was open for 0% of the time, Pallas kernels for 0%

commit v1 on v0

v1 whole, which is shorter than its diff:
```python
import jax
import jax.numpy as jnp
from jax import lax
from jax.experimental import pallas as pl
from jax.experimental.pallas import tpu as pltpu
from jax.sharding import PartitionSpec as P

MESH = pl.DeviceIdType.MESH
D = 2048
HALF = 1024
FEATS = 384
W3 = 3 * HALF
MID = W3 // 2
PIECES = (
    (0, 0), (0, 1), (1, 0), (-1, 0), (1, 1), (-1, 1), (2, 0), (-2, 0),
    (2, 1), (-2, 1), (3, 0), (-3, 0), (3, 1), (-3, 1), (4, 0), (4, 1),
)
NQ = 16
NH = 2
PER = NQ // NH
XR = PER * 4
HR = 4 * XR
RELAY = (True, False)


def kernel(
    source, w_enc, b_enc, threshold, dec_self, dec_next, target, out,
    rows, wv, bv, tv, tgt, dbuf, piece, xa, cod, cod_o, acc,
    xs, xin, relay, zs, zr, own, fin, fin_in,
    lsem, ag_s, ag_r, ax_s, ax_r, dw_s, dw_r, cx_s, cx_r, rx_s, rx_r, rz_s, rz_r, f_s, f_r,
):
    layer, feat = lax.axis_index("layer"), lax.axis_index("feat")
    zh, c = layer // 2, layer % 2
    x, y, z = feat // 16, (feat // 2) % 8, feat % 2

    def at(dx=0, dy=0, dz=0, core=None, dzh=0):
        core = c if core is None else core
        where = lax.rem(zh + dzh + 4, 4) * 2 + core
        place = lax.rem(x + dx + 4, 4) * 16 + lax.rem(y + dy + 8, 8) * 2
        return (where, place + (1 - z if dz else z))

    partner = at(core=1 - c)

    def remote(src, dst, send, recv, to):
        return pltpu.make_async_remote_copy(
            src_ref=src, dst_ref=dst, send_sem=send, recv_sem=recv, device_id=to, device_id_type=MESH
        )

    mine = pl.ds(pl.multiple_of(c * HALF, HALF), HALF)
    theirs = pl.ds(pl.multiple_of((1 - c) * HALF, HALF), HALF)
    loads = [
        pltpu.make_async_copy(source.at[0], rows, lsem.at[0]),
        pltpu.make_async_copy(w_enc.at[0], wv, lsem.at[1]),
        pltpu.make_async_copy(b_enc, bv, lsem.at[2]),
        pltpu.make_async_copy(threshold, tv, lsem.at[3]),
        pltpu.make_async_copy(dec_self.at[0, :, mine], dbuf.at[c], lsem.at[4]),
        pltpu.make_async_copy(dec_next.at[0, :, mine], dbuf.at[1 - c], lsem.at[5]),
        pltpu.make_async_copy(target.at[0], tgt, lsem.at[6]),
    ]
    for load in loads:
        load.start()

    barrier = pltpu.get_barrier_semaphore()
    peers = [at(dy=dy, dz=dz) for dy, dz in PIECES[1:]] + [at(dx=d) for d in (1, 2, 3)]
    peers += [partner, at(core=0, dzh=-1), at(core=1, dzh=-1)]
    for peer in peers:
        pl.semaphore_signal(barrier, inc=1, device_id=peer, device_id_type=MESH)

    loads[0].wait()
    r = rows[...]
    scale = lax.rsqrt(jnp.mean(r * r, axis=1, keepdims=True) + 1e-05)
    piece[0] = (r * scale).astype(jnp.bfloat16)
    pl.semaphore_wait(barrier, len(peers))

    sent = []

    def go(copy):
        copy.start()
        sent.append(copy)
        return copy

    gather = [None] + [
        remote(piece.at[0], piece.at[q], ag_s.at[q], ag_r.at[q], at(dy=PIECES[q][0], dz=PIECES[q][1]))
        for q in range(1, NQ)
    ]
    for q in reversed(range(1, NQ)):
        go(gather[q])
    lent = [
        remote(dec_self.at[0, :, theirs], dbuf.at[3 - c], dw_s.at[0], dw_r.at[0], partner),
        remote(dec_next.at[0, :, theirs], dbuf.at[2 + c], dw_s.at[1], dw_r.at[1], partner),
    ]
    for copy in lent:
        go(copy)

    spread = []
    for h in range(NH):
        for q in range(h * PER, (h + 1) * PER):
            if q:
                gather[q].wait_recv()
        block = jnp.concatenate([piece[q] for q in range(h * PER, (h + 1) * PER)], axis=0)
        xa[h, 0:XR, :] = block
        mineblock = xa.at[h, 0:XR]
        nxt = remote(mineblock, xa.at[h, 3 * XR:4 * XR], ax_s.at[h, 0], ax_r.at[h, 0], at(dx=1))
        prv = remote(mineblock, xa.at[h, XR:2 * XR], ax_s.at[h, 1], ax_r.at[h, 1], at(dx=-1))
        if RELAY[h]:
            a = remote(
                xa.at[h, 3 * XR:4 * XR, 0:HALF], xa.at[h, 2 * XR:3 * XR, 0:HALF],
                ax_s.at[h, 2], ax_r.at[h, 2], at(dx=1),
            )
            b = remote(
                xa.at[h, XR:2 * XR, HALF:D], xa.at[h, 2 * XR:3 * XR, HALF:D],
                ax_s.at[h, 3], ax_r.at[h, 3], at(dx=-1),
            )
            go(nxt)
            go(prv)
            spread.append((nxt, prv, a, b))
        else:
            opp = remote(mineblock, xa.at[h, 2 * XR:3 * XR], ax_s.at[h, 2], ax_r.at[h, 2], at(dx=2))
            go(opp)
            go(nxt)
            go(prv)
            spread.append((nxt, prv, opp))

    def relays(h):
        if RELAY[h]:
            nxt, prv, a, b = spread[h]
            nxt.wait_recv()
            go(a)
            prv.wait_recv()
            go(b)

    def arrived(h):
        if RELAY[h]:
            spread[h][2].wait_recv()
            spread[h][3].wait_recv()
        else:
            for copy in spread[h]:
                copy.wait_recv()

    def encode(h):
        pre = jnp.dot(xa[h], wv[...], preferred_element_type=jnp.float32) + bv[...]
        cod[h] = (pre * jax.nn.sigmoid((pre - tv[...]) / 0.1)).astype(jnp.bfloat16)
        copy = remote(cod.at[h], cod_o.at[h], cx_s.at[h], cx_r.at[h], partner)
        return go(copy)

    def scatter_x(h):
        def part(d, lo, hi):
            return acc[h, d * XR:(d + 1) * XR, lo:hi]

        xs[h, 0] = part(2, 0, MID).astype(jnp.bfloat16)
        xs[h, 1] = part(2, MID, W3).astype(jnp.bfloat16)
        far = [
            go(remote(xs.at[h, 0], xin.at[h, 0], rx_s.at[h, 0], rx_r.at[h, 0], at(dx=1))),
            go(remote(xs.at[h, 1], xin.at[h, 1], rx_s.at[h, 1], rx_r.at[h, 1], at(dx=-1))),
        ]
        xs[h, 2] = part(1, MID, W3).astype(jnp.bfloat16)
        xs[h, 3] = part(3, 0, MID).astype(jnp.bfloat16)
        near = [
            go(remote(xs.at[h, 2], xin.at[h, 2], rx_s.at[h, 2], rx_r.at[h, 2], at(dx=1))),
            go(remote(xs.at[h, 3], xin.at[h, 3], rx_s.at[h, 3], rx_r.at[h, 3], at(dx=-1))),
        ]
        return far, near

    def relay_x(h, far):
        out_ = []
        for i, (d, lo, hi) in enumerate(((1, 0, MID), (3, MID, W3))):
            far[i].wait_recv()
            relay[h, i] = (acc[h, d * XR:(d + 1) * XR, lo:hi] + xin[h, i].astype(jnp.float32)).astype(jnp.bfloat16)
            out_.append(
                go(remote(relay.at[h, i], xin.at[h, 4 + i], rx_s.at[h, 4 + i], rx_r.at[h, 4 + i], at(dx=1 if i == 0 else -1)))
            )
        return out_

    def scatter_zy(h, near, last):
        for copy in near + last:
            copy.wait_recv()
        f = jnp.float32
        left = acc[h, 0:XR, 0:MID] + (xin[h, 4].astype(f) + xin[h, 3].astype(f))
        right = acc[h, 0:XR, MID:W3] + (xin[h, 2].astype(f) + xin[h, 5].astype(f))
        for i in range(PER):
            q = h * PER + i
            if q == 0:
                own[:, 0:MID] = left[0:4]
                own[:, MID:W3] = right[0:4]
                continue
            zs[q, :, 0:MID] = left[4 * i:4 * i + 4].astype(jnp.bfloat16)
            zs[q, :, MID:W3] = right[4 * i:4 * i + 4].astype(jnp.bfloat16)
        copies = []
        for i in reversed(range(PER)):
            q = h * PER + i
            if q:
                dy, dz = PIECES[q]
                copies.append((q, go(remote(zs.at[q], zr.at[q], rz_s.at[q], rz_r.at[q], at(dy=-dy, dz=dz)))))
        return copies

    relays(0)
    for i in (1, 2, 3):
        loads[i].wait()
    arrived(0)
    codes = [encode(0)]
    loads[4].wait()
    loads[5].wait()
    acc[0, :, 0:HALF] = jnp.dot(cod[0], dbuf[0], preferred_element_type=jnp.float32)
    for copy in lent:
        copy.wait_recv()

    def decode(h, first):
        if first:
            acc[h, :, 0:HALF] = jnp.dot(cod[h], dbuf[0], preferred_element_type=jnp.float32)
        near_part = jnp.dot(cod[h], dbuf[1], preferred_element_type=jnp.float32)
        codes[h].wait_recv()
        acc[h, :, HALF:2 * HALF] = near_part + jnp.dot(cod_o[h], dbuf[2], preferred_element_type=jnp.float32)
        acc[h, :, 2 * HALF:W3] = jnp.dot(cod_o[h], dbuf[3], preferred_element_type=jnp.float32)

    decode(0, False)
    far0, near0 = scatter_x(0)
    relays(1)
    arrived(1)
    codes.append(encode(1))
    last0 = relay_x(0, far0)
    decode(1, True)
    far1, near1 = scatter_x(1)
    z0 = scatter_zy(0, near0, last0)
    last1 = relay_x(1, far1)
    z1 = scatter_zy(1, near1, last1)

    total = own[...]
    for q, copy in z0 + z1:
        copy.wait_recv()
        total = total + zr[q].astype(jnp.float32)
    fin[0] = total[:, 0:HALF]
    fin[1] = total[:, HALF:2 * HALF]
    fin[2] = total[:, 2 * HALF:W3]

    to_partner = remote(fin.at[1 + c], fin_in.at[0], f_s.at[0], f_r.at[0], partner)
    to_partner.start()
    onward = remote(fin.at[2 * (1 - c)], fin_in.at[1 + c], f_s.at[1], f_r.at[1 + c], at(core=0, dzh=1))
    onward.start()
    loads[6].wait()
    to_partner.wait_recv()

    @pl.when(c == 0)
    def _():
        for i in range(2):
            remote(fin.at[0], fin_in.at[1 + i], f_s.at[1], f_r.at[1 + i], partner).wait_recv()
        got0 = jnp.where(zh == 0, 0.0, fin_in[1])
        got1 = jnp.where(zh == 0, 0.0, fin_in[2])
        out[0, :, 0:HALF] = fin[0] + got0 - tgt[:, 0:HALF]
        out[0, :, HALF:D] = fin_in[0] + got1 - tgt[:, HALF:D]

    @pl.when(c == 1)
    def _():
        out[0, :, 0:HALF] = fin_in[0] - tgt[:, 0:HALF]
        out[0, :, HALF:D] = fin[1] - tgt[:, HALF:D]

    to_partner.wait_send()
    onward.wait_send()
    for copy in sent:
        copy.wait_send()


def body(*args):
    f32, bf16 = jnp.float32, jnp.bfloat16
    dma = pltpu.SemaphoreType.DMA
    v = pltpu.VMEM
    return pl.pallas_call(
        kernel,
        out_shape=jax.ShapeDtypeStruct((1, 4, D), f32),
        in_specs=[pl.BlockSpec(memory_space=pl.ANY)] * 7,
        out_specs=pl.BlockSpec(memory_space=pltpu.VMEM),
        scratch_shapes=[
            v((4, D), f32),
            v((D, FEATS), bf16),
            v((1, FEATS), f32),
            v((1, FEATS), f32),
            v((4, D), f32),
            v((4, FEATS, HALF), bf16),
            v((NQ, 4, D), bf16),
            v((NH, HR, D), bf16),
            v((NH, HR, FEATS), bf16),
            v((NH, HR, FEATS), bf16),
            v((NH, HR, W3), f32),
            v((NH, 4, XR, MID), bf16),
            v((NH, 6, XR, MID), bf16),
            v((NH, 2, XR, MID), bf16),
            v((NQ, 4, W3), bf16),
            v((NQ, 4, W3), bf16),
            v((4, W3), f32),
            v((3, 4, HALF), f32),
            v((3, 4, HALF), f32),
            dma((7,)), dma((NQ,)), dma((NQ,)), dma((NH, 4)), dma((NH, 4)), dma((2,)), dma((2,)),
            dma((NH,)), dma((NH,)), dma((NH, 6)), dma((NH, 6)), dma((NQ,)), dma((NQ,)), dma((2,)), dma((3,)),
        ],
        compiler_params=pltpu.CompilerParams(
            collective_id=0, has_side_effects=True, vmem_limit_bytes=56 * 2**20
        ),
    )(*args)


def solution(mesh):
    return jax.shard_map(
        body,
        mesh=mesh,
        in_specs=(
            P("layer", "feat", None),
            P("layer", None, "feat"),
            P("layer", "feat"),
            P("layer", "feat"),
            P("layer", "feat", None),
            P("layer", "feat", None),
            P("layer", "feat", None),
        ),
        out_specs=P("layer", "feat", None),
        check_vma=False,
    )
```

time: 962 us -> 68.2 us (0.07)
  the two profiles are of different devices: /device:TPU:1 before, /device:TPU:8 now
where the time goes in v1:
time: 68.2 us; the launch traced here: 68 us
  Pallas kernels  66.6 us (98%)
  local copies, waits for them, and re-layouts  1.38 us (2%)
    pallas_call x1, Pallas kernels, body(): pl.pallas_call(kernel, out_shape=jax.ShapeDtypeStruct((1, 4, D), f32), in...  66.6 us
    unnamed x1, local copies, waits for them, and re-layouts  1.38 us

profile of v1, /device:TPU:8, one launch (start us, length us, event | category | flops | bytes accessed | tf_op | source)
XLA Modules:
  0.0 68.0 jit_solution(13126768671796778341)
XLA Ops:
  0.0 66.6 %shard_map.73 = f32[1,4,2048]{2,1,0:T(4,128)} custom-call(f32[1,4,2048]{2,1,0:T(4,128)} %source.1, bf16[1,2048,384]{2,1,0:T(8,128)(2,1)} %w_enc.1, f32[1,384]{1,0:T(1,128)} %b_enc.1, f32[1,384]{1,0:T(1,128)} %threshold.1, bf16[1,384,2048]{2,1,0:T(8,128)(2,1)} %dec_self.1, bf16[1,384,2048]{2,1,0:T(8,128)(2,1)} %dec_next.1, f32[1,4,2048]{2,1,0:T(4,128)} %target.1), custom_call_target="tpu_custom_call" | custom-call | tf_op jit(solution)/shard_map/pallas_call | solution.py:266
  66.7 1.4 %copy.9 = f32[1,4,2048]{2,1,0:T(4,128)} copy(f32[1,4,2048]{2,1,0:T(4,128)} %shard_map.73) | data formatting | bytes 65536

commit v2 on v1

v2 whole, which is shorter than its diff:
```python
import jax
import jax.numpy as jnp
from jax import lax
from jax.experimental import pallas as pl
from jax.experimental.pallas import tpu as pltpu
from jax.sharding import PartitionSpec as P

MESH = pl.DeviceIdType.MESH
D = 2048
HALF = 1024
FEATS = 384
W3 = 3 * HALF
PIECES = (
    (4, 1), (4, 0), (3, 1), (-3, 1), (3, 0), (-3, 0), (-2, 1), (-2, 0),
    (2, 1), (1, 1), (-1, 1), (0, 1), (2, 0), (1, 0), (-1, 0), (0, 0),
)
NQ = 16
NH = 2
OWN = 15
PER = NQ // NH
XR = PER * 4
HR = 4 * XR
GROUP = 16
NG = 4
STAY = 2 * HALF
UNITS = ((1, STAY, W3, 0, XR), (0, STAY, W3, 0, XR), (0, 0, STAY, 0, XR), (1, 0, STAY, GROUP, XR))
GA = 1536
GB = D - GA
PIECES_B = ((2, 1), (2, 0), (1, 1), (3, 1), (1, 0), (3, 0), (0, 1), (0, 0))
OWN_B = 7


def kernel(
    source, w_enc, b_enc, threshold, dec_self, dec_next, target, out,
    rows, wv, bv, tv, tgt, dbuf, piece, pb, zxs, zxr, xa, cod, cod_o, acc,
    xs, xin, zs, zr, own, fin, fin_in,
    lsem, ag_s, ag_r, b1_s, b1_r, b2_s, b2_r, zx_s, zx_r, ax_s, ax_r, dw_s, dw_r, cx_s, cx_r, rx_s, rx_r, rz_s, rz_r, f_s, f_r,
):
    layer, feat = lax.axis_index("layer"), lax.axis_index("feat")
    zh, c = layer // 2, layer % 2
    x, y, z = feat // 16, (feat // 2) % 8, feat % 2

    def at(dx=0, dy=0, dz=0, core=None, dzh=0):
        core = c if core is None else core
        where = lax.rem(zh + dzh + 4, 4) * 2 + core
        place = lax.rem(x + dx + 4, 4) * 16 + lax.rem(y + dy + 8, 8) * 2
        return (where, place + (1 - z if dz else z))

    partner = at(core=1 - c)

    def remote(src, dst, send, recv, to):
        return pltpu.make_async_remote_copy(
            src_ref=src, dst_ref=dst, send_sem=send, recv_sem=recv, device_id=to, device_id_type=MESH
        )

    mine = pl.ds(pl.multiple_of(c * HALF, HALF), HALF)
    theirs = pl.ds(pl.multiple_of((1 - c) * HALF, HALF), HALF)
    loads = [
        pltpu.make_async_copy(source.at[0], rows, lsem.at[0]),
        pltpu.make_async_copy(w_enc.at[0], wv, lsem.at[1]),
        pltpu.make_async_copy(b_enc, bv, lsem.at[2]),
        pltpu.make_async_copy(threshold, tv, lsem.at[3]),
        pltpu.make_async_copy(dec_self.at[0, :, mine], dbuf.at[c], lsem.at[4]),
        pltpu.make_async_copy(dec_next.at[0, :, mine], dbuf.at[1 - c], lsem.at[5]),
        pltpu.make_async_copy(target.at[0], tgt, lsem.at[6]),
    ]
    for load in loads:
        load.start()

    barrier = pltpu.get_barrier_semaphore()
    peers = [at(dy=dy, dz=dz) for dy, dz in PIECES[:OWN]] + [partner]
    peers += [at(dx=dx, dz=dz) for dx, dz in PIECES_B if dx]
    peers += [at(dy=dy, dz=dz, dzh=-1) for dy, dz in PIECES]
    for peer in peers:
        pl.semaphore_signal(barrier, inc=1, device_id=peer, device_id_type=MESH)

    loads[0].wait()
    r = rows[...]
    scale = lax.rsqrt(jnp.mean(r * r, axis=1, keepdims=True) + 1e-05)
    normed = (r * scale).astype(jnp.bfloat16)
    piece[OWN] = normed[:, 0:GA]
    pb[0, OWN_B] = normed[:, GA:D]
    pl.semaphore_wait(barrier, len(peers))

    sent = []

    def go(copy):
        copy.start()
        sent.append(copy)
        return copy

    gather = [
        remote(piece.at[OWN], piece.at[q], ag_s.at[q], ag_r.at[q], at(dy=PIECES[q][0], dz=PIECES[q][1]))
        for q in range(OWN)
    ]
    gather_b = [
        remote(pb.at[0, OWN_B], pb.at[0, p], b1_s.at[p], b1_r.at[p], at(dx=PIECES_B[p][0], dz=PIECES_B[p][1]))
        for p in range(OWN_B)
    ]
    for q in reversed(range(OWN)):
        go(gather[q])
    for copy in gather_b:
        go(copy)
    lent = [
        remote(dec_self.at[0, :, theirs], dbuf.at[3 - c], dw_s.at[0], dw_r.at[0], partner),
        remote(dec_next.at[0, :, theirs], dbuf.at[2 + c], dw_s.at[1], dw_r.at[1], partner),
    ]
    for copy in lent:
        go(copy)

    spread = {}
    for g in reversed(range(NG)):
        for q in range(g * 4, g * 4 + 4):
            if q != OWN:
                gather[q].wait_recv()
        h, r0 = g // 2, (g % 2) * GROUP
        xa[h, r0:r0 + GROUP, 0:GA] = jnp.concatenate([piece[q] for q in range(g * 4, g * 4 + 4)], axis=0)
        block = xa.at[h, r0:r0 + GROUP, 0:GA]
        spread[g] = [
            go(remote(block, xa.at[h, pl.ds((4 - d) * XR + r0, GROUP), 0:GA], ax_s.at[g, d], ax_r.at[g, d], at(dx=d)))
            for d in (2, 1, 3)
        ]
        if g == NG - 1:
            for copy in gather_b:
                copy.wait_recv()
            spread_b = {
                dy: go(remote(pb.at[0], pb.at[8 - dy], b2_s.at[dy], b2_r.at[8 - dy], at(dy=dy)))
                for dy in (1, 7, 2, 6, 3, 5, 4)
            }

    def arrived(h):
        for g in (2 * h + 1, 2 * h):
            for copy in spread[g]:
                copy.wait_recv()
        for dy in {1: (2, 1, 7), 0: (3, 4, 5, 6)}[h]:
            spread_b[dy].wait_recv()
        for dx in range(4):
            for k in range(2):
                rows_b = []
                for q in range(h * PER + 4 * k, h * PER + 4 * k + 4):
                    dy, dz = PIECES[q]
                    rows_b.append(pb[-dy % 8, PIECES_B.index((-dx % 4, dz))])
                r0 = dx * XR + k * GROUP
                xa[h, r0:r0 + GROUP, GA:D] = jnp.concatenate(rows_b, axis=0)

    def encode(h):
        pre = jnp.dot(xa[h], wv[...], preferred_element_type=jnp.float32) + bv[...]
        cod[h] = (pre * jax.nn.sigmoid((pre - tv[...]) / 0.1)).astype(jnp.bfloat16)
        copy = remote(cod.at[h], cod_o.at[h], cx_s.at[h], cx_r.at[h], partner)
        return go(copy)

    def unit(u):
        h, lo, hi, r0, r1 = UNITS[u]
        return h, lo, (lo + hi) // 2, hi, r0, r1, (r1 - r0, (hi - lo) // 2)

    def toward(u, i, value, size):
        n, wide = size
        src = xs.at[u, i, 0:n, 0:wide]
        xs[u, i, 0:n, 0:wide] = value.astype(jnp.bfloat16)
        return go(remote(
            src, xin.at[u, i, 0:n, 0:wide], rx_s.at[u, i], rx_r.at[u, i], at(dx=1 if i % 2 == 0 else -1)
        ))

    def part(u, d, lo, hi):
        h, _, _, _, r0, r1, _ = unit(u)
        return acc[h, d * XR + r0:d * XR + r1, lo:hi]

    def scatter_far(u):
        h, lo, mid, hi, r0, r1, size = unit(u)
        return [toward(u, 0, part(u, 2, lo, mid), size), toward(u, 1, part(u, 2, mid, hi), size)]

    def scatter_near(u):
        h, lo, mid, hi, r0, r1, size = unit(u)
        return [toward(u, 2, part(u, 1, mid, hi), size), toward(u, 3, part(u, 3, lo, mid), size)]

    def came_x(u, i):
        n, wide = unit(u)[-1]
        return xin[u, i, 0:n, 0:wide].astype(jnp.float32)

    def relay_x(u, far):
        h, lo, mid, hi, r0, r1, size = unit(u)
        out_ = []
        for i, (d, p, e) in enumerate(((1, lo, mid), (3, mid, hi))):
            far[i].wait_recv()
            out_.append(toward(u, 4 + i, part(u, d, p, e) + came_x(u, i), size))
        return out_

    def scatter_zy(u, near, last):
        h, lo, mid, hi, r0, r1, size = unit(u)
        for copy in near + last:
            copy.wait_recv()
        left = part(u, 0, lo, mid) + (came_x(u, 4) + came_x(u, 3))
        right = part(u, 0, mid, hi) + (came_x(u, 2) + came_x(u, 5))
        copies = []
        for i in range((r1 - r0) // 4):
            q = h * PER + r0 // 4 + i
            if q == OWN and lo == 0:
                own[:, lo:mid] = left[4 * i:4 * i + 4]
                own[:, mid:hi] = right[4 * i:4 * i + 4]
                continue
            zs[q, :, lo:mid] = left[4 * i:4 * i + 4].astype(jnp.bfloat16)
            zs[q, :, mid:hi] = right[4 * i:4 * i + 4].astype(jnp.bfloat16)
            dy, dz = PIECES[q]
            kind = 0 if lo == 0 else 1
            copies.append(go(remote(
                zs.at[q, :, lo:hi], zr.at[q, :, lo:hi], rz_s.at[kind, q], rz_r.at[kind, q],
                at(dy=-dy, dz=dz, dzh=kind),
            )))
        return copies

    def z_send(dx):
        zxs[dx] = acc[1, dx * XR:dx * XR + GROUP, 0:STAY].astype(jnp.bfloat16)
        return go(remote(zxs.at[dx], zxr.at[dx], zx_s.at[dx], zx_r.at[dx], at(dz=1)))

    def z_add(dx):
        zx[dx].wait_recv()
        acc[1, dx * XR + GROUP:(dx + 1) * XR, 0:STAY] += zxr[dx].astype(jnp.float32)

    first = pl.ds(pl.multiple_of(c * STAY, HALF), HALF)
    other = pl.ds(pl.multiple_of((1 - c) * STAY, HALF), HALF)

    def decode_own(h):
        acc[h, :, first] = jnp.dot(cod[h], dbuf[0], preferred_element_type=jnp.float32)
        acc[h, :, HALF:STAY] = jnp.dot(cod[h], dbuf[1], preferred_element_type=jnp.float32)

    def decode_other(h):
        codes[h].wait_recv()
        acc[h, :, other] = jnp.dot(cod_o[h], dbuf[3], preferred_element_type=jnp.float32)
        acc[h, :, HALF:STAY] += jnp.dot(cod_o[h], dbuf[2], preferred_element_type=jnp.float32)

    codes = {}
    for i in (1, 2, 3):
        loads[i].wait()
    arrived(1)
    codes[1] = encode(1)
    loads[4].wait()
    loads[5].wait()
    decode_own(1)
    for copy in lent:
        copy.wait_recv()
    decode_other(1)
    far, near, last, zy = {}, {}, {}, {}
    far[0] = scatter_far(0)
    near[0] = scatter_near(0)
    zx = {dx: z_send(dx) for dx in (2, 1, 3, 0)}
    arrived(0)
    codes[0] = encode(0)
    decode_own(0)
    decode_other(0)
    far[1] = scatter_far(1)
    near[1] = scatter_near(1)
    far[2] = scatter_far(2)
    last[0] = relay_x(0, far[0])
    near[2] = scatter_near(2)
    last[1] = relay_x(1, far[1])
    z_add(2)
    far[3] = scatter_far(3)
    last[2] = relay_x(2, far[2])
    z_add(1)
    z_add(3)
    near[3] = scatter_near(3)
    zy[0] = scatter_zy(0, near[0], last[0])
    zy[1] = scatter_zy(1, near[1], last[1])
    last[3] = relay_x(3, far[3])
    z_add(0)
    zy[2] = scatter_zy(2, near[2], last[2])
    zy[3] = scatter_zy(3, near[3], last[3])

    def gathered(total, copies, u):
        h, lo, hi, r0, r1 = UNITS[u]
        for copy in copies:
            copy.wait_recv()
        for q in range(h * PER + r0 // 4, h * PER + r1 // 4):
            if q != OWN or lo:
                total = total + zr[q, :, lo:hi].astype(jnp.float32)
        return total

    stay = gathered(own[...], zy[2], 2)
    came = gathered(jnp.zeros((4, HALF), jnp.float32), zy[0], 0)
    came = gathered(came, zy[1], 1)
    stay = gathered(stay, zy[3], 3)
    fin[0] = stay[:, 0:HALF] + jnp.where(zh == 0, 0.0, came)
    fin[1] = stay[:, HALF:STAY]
    loads[6].wait()
    swap = remote(fin.at[1 - c], fin_in.at[0], f_s.at[0], f_r.at[0], partner)
    swap.start()
    out[0, :, mine] = fin[c] - tgt[:, mine]
    swap.wait_recv()
    out[0, :, theirs] = fin_in[0] - tgt[:, theirs]
    swap.wait_send()
    for copy in sent:
        copy.wait_send()


def body(*args):
    f32, bf16 = jnp.float32, jnp.bfloat16
    dma = pltpu.SemaphoreType.DMA
    v = pltpu.VMEM
    return pl.pallas_call(
        kernel,
        out_shape=jax.ShapeDtypeStruct((1, 4, D), f32),
        in_specs=[pl.BlockSpec(memory_space=pl.ANY)] * 7,
        out_specs=pl.BlockSpec(memory_space=pltpu.VMEM),
        scratch_shapes=[
            v((4, D), f32),
            v((D, FEATS), bf16),
            v((1, FEATS), f32),
            v((1, FEATS), f32),
            v((4, D), f32),
            v((4, FEATS, HALF), bf16),
            v((NQ, 4, GA), bf16),
            v((8, 8, 4, GB), bf16),
            v((4, GROUP, STAY), bf16),
            v((4, GROUP, STAY), bf16),
            v((NH, HR, D), bf16),
            v((NH, HR, FEATS), bf16),
            v((NH, HR, FEATS), bf16),
            v((NH, HR, W3), f32),
            v((4, 6, XR, HALF), bf16),
            v((4, 6, XR, HALF), bf16),
            v((NQ, 4, W3), bf16),
            v((NQ, 4, W3), bf16),
            v((4, STAY), f32),
            v((2, 4, HALF), f32),
            v((1, 4, HALF), f32),
            dma((7,)), dma((NQ,)), dma((NQ,)), dma((8,)), dma((8,)), dma((8,)), dma((8,)), dma((4,)), dma((4,)), dma((NG, 4)), dma((NG, 4)), dma((2,)), dma((2,)),
            dma((NH,)), dma((NH,)), dma((4, 6)), dma((4, 6)), dma((2, NQ)), dma((2, NQ)), dma((1,)), dma((1,)),
        ],
        compiler_params=pltpu.CompilerParams(
            collective_id=0, has_side_effects=True, vmem_limit_bytes=56 * 2**20
        ),
    )(*args)


def solution(mesh):
    return jax.shard_map(
        body,
        mesh=mesh,
        in_specs=(
            P("layer", "feat", None),
            P("layer", None, "feat"),
            P("layer", "feat"),
            P("layer", "feat"),
            P("layer", "feat", None),
            P("layer", "feat", None),
            P("layer", "feat", None),
        ),
        out_specs=P("layer", "feat", None),
        check_vma=False,
    )
```

time: 68.2 us -> 53.1 us (0.78)
  the two profiles are of different devices: /device:TPU:8 before, /device:TPU:1 now
where the time goes in v2:
time: 53.1 us; the launch traced here: 52.9 us
  Pallas kernels  51.5 us (97%)
  local copies, waits for them, and re-layouts  1.38 us (3%)
    pallas_call x1, Pallas kernels, body(): pl.pallas_call(kernel, out_shape=jax.ShapeDtypeStruct((1, 4, D), f32), in...  51.5 us
    unnamed x1, local copies, waits for them, and re-layouts  1.38 us

profile of v2, /device:TPU:1, one launch (start us, length us, event | category | flops | bytes accessed | tf_op | source)
XLA Modules:
  0.0 52.9 jit_solution(1322624529318280905)
XLA Ops:
  0.0 51.5 %shard_map.73 = f32[1,4,2048]{2,1,0:T(4,128)} custom-call(f32[1,4,2048]{2,1,0:T(4,128)} %source.1, bf16[1,2048,384]{2,1,0:T(8,128)(2,1)} %w_enc.1, f32[1,384]{1,0:T(1,128)} %b_enc.1, f32[1,384]{1,0:T(1,128)} %threshold.1, bf16[1,384,2048]{2,1,0:T(8,128)(2,1)} %dec_self.1, bf16[1,384,2048]{2,1,0:T(8,128)(2,1)} %dec_next.1, f32[1,4,2048]{2,1,0:T(4,128)} %target.1), custom_call_target="tpu_custom_call" | custom-call | tf_op jit(solution)/shard_map/pallas_call | solution.py:299
  51.5 1.4 %copy.9 = f32[1,4,2048]{2,1,0:T(4,128)} copy(f32[1,4,2048]{2,1,0:T(4,128)} %shard_map.73) | data formatting | bytes 65536

commit v3 on v2

--- a/solution.py
+++ b/solution.py
@@ -82,58 +82,49 @@
     pb[0, OWN_B] = normed[:, GA:D]
     pl.semaphore_wait(barrier, len(peers))
 
-    sent = []
-
     def go(copy):
         copy.start()
-        sent.append(copy)
         return copy
 
-    gather = [
-        remote(piece.at[OWN], piece.at[q], ag_s.at[q], ag_r.at[q], at(dy=PIECES[q][0], dz=PIECES[q][1]))
-        for q in range(OWN)
-    ]
+    def take(ref, sem):
+        pltpu.make_async_copy(ref, ref, sem).wait()
+
+    direct = range(OWN)
+    gather = {
+        q: remote(piece.at[OWN], piece.at[q], ag_s.at[0], ag_r.at[q // 4], at(dy=PIECES[q][0], dz=PIECES[q][1]))
+        for q in direct
+    }
     gather_b = [
-        remote(pb.at[0, OWN_B], pb.at[0, p], b1_s.at[p], b1_r.at[p], at(dx=PIECES_B[p][0], dz=PIECES_B[p][1]))
+        remote(pb.at[0, OWN_B], pb.at[0, p], b1_s.at[0], b1_r.at[0], at(dx=PIECES_B[p][0], dz=PIECES_B[p][1]))
         for p in range(OWN_B)
     ]
-    for q in reversed(range(OWN)):
+    for q in reversed(direct):
         go(gather[q])
     for copy in gather_b:
         go(copy)
     lent = [
         remote(dec_self.at[0, :, theirs], dbuf.at[3 - c], dw_s.at[0], dw_r.at[0], partner),
-        remote(dec_next.at[0, :, theirs], dbuf.at[2 + c], dw_s.at[1], dw_r.at[1], partner),
+        remote(dec_next.at[0, :, theirs], dbuf.at[2 + c], dw_s.at[0], dw_r.at[0], partner),
     ]
     for copy in lent:
         go(copy)
 
-    spread = {}
-    for g in reversed(range(NG)):
-        for q in range(g * 4, g * 4 + 4):
-            if q != OWN:
-                gather[q].wait_recv()
+    for g in (3, 2, 1, 0):
+        take(piece.at[4 * g:min(4 * g + 4, OWN)], ag_r.at[g])
         h, r0 = g // 2, (g % 2) * GROUP
         xa[h, r0:r0 + GROUP, 0:GA] = jnp.concatenate([piece[q] for q in range(g * 4, g * 4 + 4)], axis=0)
         block = xa.at[h, r0:r0 + GROUP, 0:GA]
-        spread[g] = [
-            go(remote(block, xa.at[h, pl.ds((4 - d) * XR + r0, GROUP), 0:GA], ax_s.at[g, d], ax_r.at[g, d], at(dx=d)))
-            for d in (2, 1, 3)
-        ]
+        for d in (2, 1, 3):
+            go(remote(block, xa.at[h, pl.ds((4 - d) * XR + r0, GROUP), 0:GA], ax_s.at[0], ax_r.at[h], at(dx=d)))
         if g == NG - 1:
-            for copy in gather_b:
-                copy.wait_recv()
-            spread_b = {
-                dy: go(remote(pb.at[0], pb.at[8 - dy], b2_s.at[dy], b2_r.at[8 - dy], at(dy=dy)))
-                for dy in (1, 7, 2, 6, 3, 5, 4)
-            }
+            take(pb.at[0, 0:OWN_B], b1_r.at[0])
+            for dy in (1, 7, 2, 6, 3, 5, 4):
+                there = 8 - dy
+                end = b2_r.at[0 if there in (2, 3, 4, 5) else 1]
+                go(remote(pb.at[0], pb.at[there], b2_s.at[0], end, at(dy=dy)))
 
     def arrived(h):
-        for g in (2 * h + 1, 2 * h):
-            for copy in spread[g]:
-                copy.wait_recv()
-        for dy in {1: (2, 1, 7), 0: (3, 4, 5, 6)}[h]:
-            spread_b[dy].wait_recv()
+        take(pb.at[0:3] if h else pb.at[3:7], b2_r.at[h])
         for dx in range(4):
             for k in range(2):
                 rows_b = []
@@ -142,6 +133,7 @@
                     rows_b.append(pb[-dy % 8, PIECES_B.index((-dx % 4, dz))])
                 r0 = dx * XR + k * GROUP
                 xa[h, r0:r0 + GROUP, GA:D] = jnp.concatenate(rows_b, axis=0)
+        take(xa.at[h, 0:3 * XR, 0:GA], ax_r.at[h])
 
     def encode(h):
         pre = jnp.dot(xa[h], wv[...], preferred_element_type=jnp.float32) + bv[...]
@@ -158,7 +150,7 @@
         src = xs.at[u, i, 0:n, 0:wide]
         xs[u, i, 0:n, 0:wide] = value.astype(jnp.bfloat16)
         return go(remote(
-            src, xin.at[u, i, 0:n, 0:wide], rx_s.at[u, i], rx_r.at[u, i], at(dx=1 if i % 2 == 0 else -1)
+            src, xin.at[u, i, 0:n, 0:wide], rx_s.at[u], rx_r.at[u, min(i, 2)], at(dx=1 if i % 2 == 0 else -1)
         ))
 
     def part(u, d, lo, hi):
@@ -171,7 +163,8 @@
 
     def scatter_near(u):
         h, lo, mid, hi, r0, r1, size = unit(u)
-        return [toward(u, 2, part(u, 1, mid, hi), size), toward(u, 3, part(u, 3, lo, mid), size)]
+        toward(u, 2, part(u, 1, mid, hi), size)
+        toward(u, 3, part(u, 3, lo, mid), size)
 
     def came_x(u, i):
         n, wide = unit(u)[-1]
@@ -179,19 +172,15 @@
 
     def relay_x(u, far):
         h, lo, mid, hi, r0, r1, size = unit(u)
-        out_ = []
         for i, (d, p, e) in enumerate(((1, lo, mid), (3, mid, hi))):
             far[i].wait_recv()
-            out_.append(toward(u, 4 + i, part(u, d, p, e) + came_x(u, i), size))
-        return out_
-
-    def scatter_zy(u, near, last):
+            toward(u, 4 + i, part(u, d, p, e) + came_x(u, i), size)
+
+    def scatter_zy(u):
         h, lo, mid, hi, r0, r1, size = unit(u)
-        for copy in near + last:
-            copy.wait_recv()
+        take(xin.at[u, 2:6, 0:size[0], 0:size[1]], rx_r.at[u, 2])
         left = part(u, 0, lo, mid) + (came_x(u, 4) + came_x(u, 3))
         right = part(u, 0, mid, hi) + (came_x(u, 2) + came_x(u, 5))
-        copies = []
         for i in range((r1 - r0) // 4):
             q = h * PER + r0 // 4 + i
             if q == OWN and lo == 0:
@@ -202,15 +191,14 @@
             zs[q, :, mid:hi] = right[4 * i:4 * i + 4].astype(jnp.bfloat16)
             dy, dz = PIECES[q]
             kind = 0 if lo == 0 else 1
-            copies.append(go(remote(
-                zs.at[q, :, lo:hi], zr.at[q, :, lo:hi], rz_s.at[kind, q], rz_r.at[kind, q],
+            go(remote(
+                zs.at[q, :, lo:hi], zr.at[q, :, lo:hi], rz_s.at[u], rz_r.at[u],
                 at(dy=-dy, dz=dz, dzh=kind),
-            )))
-        return copies
+            ))
 
     def z_send(dx):
         zxs[dx] = acc[1, dx * XR:dx * XR + GROUP, 0:STAY].astype(jnp.bfloat16)
-        return go(remote(zxs.at[dx], zxr.at[dx], zx_s.at[dx], zx_r.at[dx], at(dz=1)))
+        return go(remote(zxs.at[dx], zxr.at[dx], zx_s.at[0], zx_r.at[dx], at(dz=1)))
 
     def z_add(dx):
         zx[dx].wait_recv()
@@ -226,59 +214,71 @@
     def decode_other(h):
         codes[h].wait_recv()
         acc[h, :, other] = jnp.dot(cod_o[h], dbuf[3], preferred_element_type=jnp.float32)
+
+    def decode_mixed(h):
         acc[h, :, HALF:STAY] += jnp.dot(cod_o[h], dbuf[2], preferred_element_type=jnp.float32)
 
     codes = {}
     for i in (1, 2, 3):
         loads[i].wait()
+    far, zx = {}, {}
     arrived(1)
     codes[1] = encode(1)
     loads[4].wait()
     loads[5].wait()
     decode_own(1)
-    for copy in lent:
-        copy.wait_recv()
+    take(dbuf.at[0:2], dw_r.at[0])
     decode_other(1)
-    far, near, last, zy = {}, {}, {}, {}
     far[0] = scatter_far(0)
-    near[0] = scatter_near(0)
-    zx = {dx: z_send(dx) for dx in (2, 1, 3, 0)}
+    scatter_near(0)
+    decode_mixed(1)
+    for dx in (2, 1, 3, 0):
+        zx[dx] = z_send(dx)
     arrived(0)
     codes[0] = encode(0)
     decode_own(0)
     decode_other(0)
     far[1] = scatter_far(1)
-    near[1] = scatter_near(1)
+    scatter_near(1)
+    decode_mixed(0)
     far[2] = scatter_far(2)
-    last[0] = relay_x(0, far[0])
-    near[2] = scatter_near(2)
-    last[1] = relay_x(1, far[1])
+    relay_x(0, far[0])
+    scatter_near(2)
+    relay_x(1, far[1])
+    scatter_zy(0)
     z_add(2)
     far[3] = scatter_far(3)
-    last[2] = relay_x(2, far[2])
+    relay_x(2, far[2])
     z_add(1)
     z_add(3)
-    near[3] = scatter_near(3)
-    zy[0] = scatter_zy(0, near[0], last[0])
-    zy[1] = scatter_zy(1, near[1], last[1])
-    last[3] = relay_x(3, far[3])
+    scatter_near(3)
+    scatter_zy(1)
+    relay_x(3, far[3])
+    scatter_zy(2)
     z_add(0)
-    zy[2] = scatter_zy(2, near[2], last[2])
-    zy[3] = scatter_zy(3, near[3], last[3])
-
-    def gathered(total, copies, u):
+    scatter_zy(3)
+    take(piece.at[0:OWN], ag_s.at[0])
+    take(pb.at[0, 0:OWN_B], b1_s.at[0])
+    take(pb.at[0:7], b2_s.at[0])
+    take(xa.at[:, 0:3 * XR, 0:GA], ax_s.at[0])
+    take(dbuf.at[0:2], dw_s.at[0])
+    take(zxs, zx_s.at[0])
+    for h in range(NH):
+        codes[h].wait_send()
+
+    def gathered(total, u):
         h, lo, hi, r0, r1 = UNITS[u]
-        for copy in copies:
-            copy.wait_recv()
+        q0, q1 = h * PER + r0 // 4, h * PER + r1 // 4
+        take(zr.at[q0:min(q1, OWN) if lo == 0 else q1, :, lo:hi], rz_r.at[u])
         for q in range(h * PER + r0 // 4, h * PER + r1 // 4):
             if q != OWN or lo:
                 total = total + zr[q, :, lo:hi].astype(jnp.float32)
         return total
 
-    stay = gathered(own[...], zy[2], 2)
-    came = gathered(jnp.zeros((4, HALF), jnp.float32), zy[0], 0)
-    came = gathered(came, zy[1], 1)
-    stay = gathered(stay, zy[3], 3)
+    came = gathered(jnp.zeros((4, HALF), jnp.float32), 0)
+    came = gathered(came, 1)
+    stay = gathered(own[...], 3)
+    stay = gathered(stay, 2)
     fin[0] = stay[:, 0:HALF] + jnp.where(zh == 0, 0.0, came)
     fin[1] = stay[:, HALF:STAY]
     loads[6].wait()
@@ -288,8 +288,11 @@
     swap.wait_recv()
     out[0, :, theirs] = fin_in[0] - tgt[:, theirs]
     swap.wait_send()
-    for copy in sent:
-        copy.wait_send()
+    for u in range(4):
+        h, lo, mid, hi, r0, r1, (n, wide) = unit(u)
+        q0, q1 = h * PER + r0 // 4, h * PER + r1 // 4
+        take(xs.at[u, :, 0:n, 0:wide], rx_s.at[u])
+        take(zs.at[q0:min(q1, OWN) if lo == 0 else q1, :, lo:hi], rz_s.at[u])
 
 
 def body(*args):
@@ -323,8 +326,9 @@
             v((4, STAY), f32),
             v((2, 4, HALF), f32),
             v((1, 4, HALF), f32),
-            dma((7,)), dma((NQ,)), dma((NQ,)), dma((8,)), dma((8,)), dma((8,)), dma((8,)), dma((4,)), dma((4,)), dma((NG, 4)), dma((NG, 4)), dma((2,)), dma((2,)),
-            dma((NH,)), dma((NH,)), dma((4, 6)), dma((4, 6)), dma((2, NQ)), dma((2, NQ)), dma((1,)), dma((1,)),
+            dma((7,)), dma((1,)), dma((NG,)), dma((1,)), dma((1,)), dma((1,)), dma((NH,)), dma((1,)), dma((4,)),
+            dma((1,)), dma((NH,)), dma((1,)), dma((1,)), dma((NH,)), dma((NH,)), dma((4,)), dma((4, 3)),
+            dma((4,)), dma((4,)), dma((1,)), dma((1,)),
         ],
         compiler_params=pltpu.CompilerParams(
             collective_id=0, has_side_effects=True, vmem_limit_bytes=56 * 2**20

time: 53.1 us -> 50.7 us (0.955)
  Pallas kernels: 51.5 us -> 49.1 us
    pallas_call x1, Pallas kernels: 51.5 us -> 49.1 us  [body(): pl.pallas_call(kernel, out_shape=jax.ShapeDtypeStruct((1, 4, D), f32), in...]
where the time goes in v3:
time: 50.7 us; the launch traced here: 50.5 us
  Pallas kernels  49.1 us (97%)
  local copies, waits for them, and re-layouts  1.38 us (3%)
    pallas_call x1, Pallas kernels, body(): pl.pallas_call(kernel, out_shape=jax.ShapeDtypeStruct((1, 4, D), f32), in...  49.1 us
    unnamed x1, local copies, waits for them, and re-layouts  1.38 us

profile of v3, /device:TPU:1, one launch (start us, length us, event | category | flops | bytes accessed | tf_op | source)
XLA Modules:
  0.0 50.5 jit_solution(8743479068027242945)
XLA Ops:
  0.0 49.1 %shard_map.73 = f32[1,4,2048]{2,1,0:T(4,128)} custom-call(f32[1,4,2048]{2,1,0:T(4,128)} %source.1, bf16[1,2048,384]{2,1,0:T(8,128)(2,1)} %w_enc.1, f32[1,384]{1,0:T(1,128)} %b_enc.1, f32[1,384]{1,0:T(1,128)} %threshold.1, bf16[1,384,2048]{2,1,0:T(8,128)(2,1)} %dec_self.1, bf16[1,384,2048]{2,1,0:T(8,128)(2,1)} %dec_next.1, f32[1,4,2048]{2,1,0:T(4,128)} %target.1), custom_call_target="tpu_custom_call" | custom-call | tf_op jit(solution)/shard_map/pallas_call | solution.py:302
  49.1 1.4 %copy.9 = f32[1,4,2048]{2,1,0:T(4,128)} copy(f32[1,4,2048]{2,1,0:T(4,128)} %shard_map.73) | data formatting | bytes 65536

commit v4 on v3

--- a/solution.py
+++ b/solution.py
@@ -61,8 +61,8 @@
         pltpu.make_async_copy(b_enc, bv, lsem.at[2]),
         pltpu.make_async_copy(threshold, tv, lsem.at[3]),
         pltpu.make_async_copy(dec_self.at[0, :, mine], dbuf.at[c], lsem.at[4]),
-        pltpu.make_async_copy(dec_next.at[0, :, mine], dbuf.at[1 - c], lsem.at[5]),
-        pltpu.make_async_copy(target.at[0], tgt, lsem.at[6]),
+        pltpu.make_async_copy(dec_next.at[0, :, mine], dbuf.at[1 - c], lsem.at[4]),
+        pltpu.make_async_copy(target.at[0], tgt, lsem.at[5]),
     ]
     for load in loads:
         load.start()
@@ -138,7 +138,7 @@
     def encode(h):
         pre = jnp.dot(xa[h], wv[...], preferred_element_type=jnp.float32) + bv[...]
         cod[h] = (pre * jax.nn.sigmoid((pre - tv[...]) / 0.1)).astype(jnp.bfloat16)
-        copy = remote(cod.at[h], cod_o.at[h], cx_s.at[h], cx_r.at[h], partner)
+        copy = remote(cod.at[h], cod_o.at[h], cx_s.at[0], cx_r.at[h], partner)
         return go(copy)
 
     def unit(u):
@@ -224,8 +224,7 @@
     far, zx = {}, {}
     arrived(1)
     codes[1] = encode(1)
-    loads[4].wait()
-    loads[5].wait()
+    take(dbuf.at[0:2], lsem.at[4])
     decode_own(1)
     take(dbuf.at[0:2], dw_r.at[0])
     decode_other(1)
@@ -242,8 +241,8 @@
     scatter_near(1)
     decode_mixed(0)
     far[2] = scatter_far(2)
+    scatter_near(2)
     relay_x(0, far[0])
-    scatter_near(2)
     relay_x(1, far[1])
     scatter_zy(0)
     z_add(2)
@@ -263,8 +262,7 @@
     take(xa.at[:, 0:3 * XR, 0:GA], ax_s.at[0])
     take(dbuf.at[0:2], dw_s.at[0])
     take(zxs, zx_s.at[0])
-    for h in range(NH):
-        codes[h].wait_send()
+    take(cod, cx_s.at[0])
 
     def gathered(total, u):
         h, lo, hi, r0, r1 = UNITS[u]
@@ -326,8 +324,8 @@
             v((4, STAY), f32),
             v((2, 4, HALF), f32),
             v((1, 4, HALF), f32),
-            dma((7,)), dma((1,)), dma((NG,)), dma((1,)), dma((1,)), dma((1,)), dma((NH,)), dma((1,)), dma((4,)),
-            dma((1,)), dma((NH,)), dma((1,)), dma((1,)), dma((NH,)), dma((NH,)), dma((4,)), dma((4, 3)),
+            dma((6,)), dma((1,)), dma((NG,)), dma((1,)), dma((1,)), dma((1,)), dma((NH,)), dma((1,)), dma((4,)),
+            dma((1,)), dma((NH,)), dma((1,)), dma((1,)), dma((1,)), dma((NH,)), dma((4,)), dma((4, 3)),
             dma((4,)), dma((4,)), dma((1,)), dma((1,)),
         ],
         compiler_params=pltpu.CompilerParams(

time: 50.7 us -> 51.6 us (1.018)
  Pallas kernels: 49.1 us -> 50.1 us
    pallas_call x1, Pallas kernels: 49.1 us -> 50.1 us  [body(): pl.pallas_call(kernel, out_shape=jax.ShapeDtypeStruct((1, 4, D), f32), in...]
where the time goes in v4:
time: 51.6 us; the launch traced here: 51.5 us
  Pallas kernels  50.1 us (97%)
  local copies, waits for them, and re-layouts  1.38 us (3%)
    pallas_call x1, Pallas kernels, body(): pl.pallas_call(kernel, out_shape=jax.ShapeDtypeStruct((1, 4, D), f32), in...  50.1 us
    unnamed x1, local copies, waits for them, and re-layouts  1.38 us

profile of v4, /device:TPU:1, one launch (start us, length us, event | category | flops | bytes accessed | tf_op | source)
XLA Modules:
  0.0 51.5 jit_solution(18240759862561204654)
XLA Ops:
  0.0 50.1 %shard_map.73 = f32[1,4,2048]{2,1,0:T(4,128)} custom-call(f32[1,4,2048]{2,1,0:T(4,128)} %source.1, bf16[1,2048,384]{2,1,0:T(8,128)(2,1)} %w_enc.1, f32[1,384]{1,0:T(1,128)} %b_enc.1, f32[1,384]{1,0:T(1,128)} %threshold.1, bf16[1,384,2048]{2,1,0:T(8,128)(2,1)} %dec_self.1, bf16[1,384,2048]{2,1,0:T(8,128)(2,1)} %dec_next.1, f32[1,4,2048]{2,1,0:T(4,128)} %target.1), custom_call_target="tpu_custom_call" | custom-call | tf_op jit(solution)/shard_map/pallas_call | solution.py:300
  50.1 1.4 %copy.9 = f32[1,4,2048]{2,1,0:T(4,128)} copy(f32[1,4,2048]{2,1,0:T(4,128)} %shard_map.73) | data formatting | bytes 65536
